TPU v7x, 32 devices: a whole 2x2x4 slice. The times are simulated.
32 devices in a mesh: fsdp: 8 (over z, y), tp: 4 (over x, core).
Axes of the slice: x: 2, y: 2, z: 4, core: 2. Of those that a mesh axis runs over, the one named last changes fastest.
Arguments:
- activations: bfloat16 [8192, 4096], P('fsdp', 'tp'), may hold values from -6 to 6
- out_grads: bfloat16 [2, 8192, 1024], P(None, 'fsdp', 'tp'), may hold values from -0.06591797 to 0.06591797
- bases: float32 [2, 4096, 256], P(None, 'fsdp'), may hold values from -0.09375 to 0.09375
- weights: float32 [2, 4096, 1024], P(None, 'fsdp', 'tp'), may hold values from -6 to 6
- first_moment: float32 [2, 256, 1024], P(None, 'fsdp', 'tp'), may hold values from -6 to 6
- second_moment: float32 [2, 256, 1024], P(None, 'fsdp', 'tp'), may hold values from 0.01 to 1
Outputs:
- new_weights: float32 [2, 4096, 1024], P(None, 'fsdp', 'tp')
- new_first: float32 [2, 256, 1024], P(None, 'fsdp', 'tp')
- new_second: float32 [2, 256, 1024], P(None, 'fsdp', 'tp')
- new_bases: float32 [2, 4096, 256], P(None, 'fsdp')
All inputs are finite; a program needn't handle non-finite values.
Results may differ from a plain program's by a relative error of at most 0.0003.
Values may be sent and summed in bfloat16 or wider, within the bound.
A program may use at most 128 MiB of HBM per device.

v0:
```python
import jax
import jax.numpy as jnp
from jax import lax
from jax.sharding import PartitionSpec as P

NS_STEPS = 5


COEF_A = 3.4445
COEF_B = -4.775
COEF_C = 2.0315
BETA_ONE = 0.9
BETA_TWO = 0.999
CORRECT_ONE = 1.0 - 0.9**10
CORRECT_TWO = 1.0 - 0.999**10
EPSILON = 1e-08
NORM_EPS = 1e-07
RATE = 2.0


def gram_total(value):
    return lax.psum(value, "fsdp")


def norm_total(value):
    return lax.psum(value, "fsdp")


def orthogonalize(cand):
    high = lax.Precision.HIGHEST
    squared = norm_total(jnp.sum(cand * cand, axis=(0, 2)))
    scale = jnp.sqrt(squared) + NORM_EPS
    current = cand / scale[None, :, None]
    gram = gram_total(jnp.einsum("dmk,dml->mkl", current, current, precision=high))
    for step in range(NS_STEPS):
        if step > 0:
            gram = gram_total(jnp.einsum("dmk,dml->mkl", current, current, precision=high))
        mixer = COEF_B * gram + COEF_C * jnp.einsum("mkl,mlj->mkj", gram, gram, precision=high)
        current = COEF_A * current + jnp.einsum("dmk,mkl->dml", current, mixer, precision=high)
    return current


def body(activations, out_grads, bases, weights, first_moment, second_moment):
    high = lax.Precision.HIGHEST
    gathered = lax.all_gather(activations, "tp", axis=1, tiled=True)
    grad_part = lax.psum_scatter(
        jnp.einsum("tr,mtc->rmc", gathered, out_grads, preferred_element_type=jnp.float32),
        "fsdp",
        scatter_dimension=0,
        tiled=True,
    )
    projected = lax.psum(jnp.einsum("mdk,dmc->mkc", bases, grad_part, precision=high), "fsdp")
    cand_part = jnp.einsum("dmc,mkc->dmk", grad_part, projected, precision=high)
    rank_rows = first_moment.shape[1]
    start_row = lax.axis_index("fsdp") * rank_rows
    own_proj = lax.dynamic_slice_in_dim(projected, start_row, rank_rows, 1)
    new_first = BETA_ONE * first_moment + (1.0 - BETA_ONE) * own_proj
    new_second = BETA_TWO * second_moment + (1.0 - BETA_TWO) * own_proj * own_proj
    adam_step = new_first / CORRECT_ONE / (jnp.sqrt(new_second / CORRECT_TWO) + EPSILON)
    step_full = lax.all_gather(adam_step, "fsdp", axis=1, tiled=True)
    new_weights = weights - RATE * jnp.einsum("mdk,mkc->mdc", bases, step_full, precision=high)
    whole_cand = lax.psum(cand_part, "tp")
    ortho = orthogonalize(whole_cand)
    new_bases = jnp.transpose(ortho, (1, 0, 2))
    return (new_weights, new_first, new_second, new_bases)


def solution(mesh):
    return jax.shard_map(
        body,
        mesh=mesh,
        in_specs=(
            P("fsdp", "tp"),
            P(None, "fsdp", "tp"),
            P(None, "fsdp", None),
            P(None, "fsdp", "tp"),
            P(None, "fsdp", "tp"),
            P(None, "fsdp", "tp"),
        ),
        out_specs=(
            P(None, "fsdp", "tp"),
            P(None, "fsdp", "tp"),
            P(None, "fsdp", "tp"),
            P(None, "fsdp", None),
        ),
        check_vma=False,
    )
```

profile of v0, /device:TPU:0, one launch (start us, length us, event | category | flops | bytes accessed | tf_op | source)
XLA Modules:
  0.0 764.5 jit_solution(5475081602518478065)
XLA Ops:
  7.2 4.0 copy.63
  11.3 61.1 %all-gather.2.cloned.1.call-done = bf16[1024,4096]{0,1:T(8,128)(2,1)} async-done(((bf16[1024,1024]{0,1:T(8,128)(2,1)}), bf16[1024,4096]{0,1:T(8,128)(2,1)}) %all-gather.2.cloned.1.call-update) | async-done | bytes 8388624 | tf_op jit(solution)/shard_map/all_gather | solution.py:45
  72.4 10.1 %fusion = f32[4096,2,256]{2,0,1:T(8,128)} fusion(bf16[2,1024,256]{2,1,0:T(8,128)(2,1)S(1)} %copy-done, bf16[1024,4096]{0,1:T(8,128)(2,1)} %all-gather.2.cloned.1.call-done), kind=kOutput, calls=%fused_computation | convolution fusion | flops 4294967296 | bytes 17825792 | tf_op jit(solution)/shard_map/tr,mtc->rmc/dot_general | solution.py:47
  82.6 149.1 %reduce-scatter.2.cloned.1.call-done = f32[512,2,256]{2,0,1:T(8,128)} async-done(((f32[4096,2,256]{2,0,1:T(8,128)}), f32[512,2,256]{2,0,1:T(8,128)}) %reduce-scatter.2.cloned.1.call-update) | async-done | bytes 1048592 | tf_op jit(solution)/shard_map/reduce_scatter | solution.py:46
  231.7 3.9 convolution_bitcast_fusion.6
  235.7 71.9 %all-reduce.8.cloned.1.call-done = f32[2,256,256]{2,1,0:T(8,128)} async-done(((f32[2,256,256]{2,1,0:T(8,128)}), f32[2,256,256]{2,1,0:T(8,128)}) %all-reduce.8.cloned.1.call-update) | async-done | bytes 524304 | tf_op jit(solution)/shard_map/psum | solution.py:52
  307.5 3.4 convolution_bitcast_fusion.5
  311.0 35.5 %all-reduce.10.cloned.1.call-done = f32[512,2,256]{0,2,1:T(8,128)} async-done(((f32[512,2,256]{0,2,1:T(8,128)}), f32[512,2,256]{0,2,1:T(8,128)}) %all-reduce.10.cloned.1.call-update) | async-done | bytes 1048592 | tf_op jit(solution)/shard_map/psum | solution.py:62
  347.9 21.3 %psum.58 = f32[2]{0:T(128)S(1)} all-reduce(f32[2]{0:T(128)S(1)} %multiply_reduce_fusion), channel_id=1, replica_groups=mesh['fsdp'=8,'tp'=4] {'fsdp'}, use_global_device_ids=true, to_apply=%region_4.0 | all-reduce | flops 2 | bytes 16 | tf_op jit(solution)/shard_map/psum | solution.py:26
  369.3 3.6 fusion.16
  373.0 69.2 %all-reduce.12.cloned.1.call-done = f32[2,256,256]{2,1,0:T(8,128)} async-done(((f32[2,256,256]{2,1,0:T(8,128)}), f32[2,256,256]{2,1,0:T(8,128)}) %all-reduce.12.cloned.1.call-update) | async-done | bytes 524304 | tf_op jit(solution)/shard_map/psum | solution.py:22
  442.2 2.2 fusion.14
  444.4 2.9 fusion.9
  449.5 71.5 %all-reduce.14.cloned.1.call-done = f32[2,256,256]{2,1,0:T(8,128)} async-done(((f32[2,256,256]{2,1,0:T(8,128)}), f32[2,256,256]{2,1,0:T(8,128)}) %all-reduce.14.cloned.1.call-update) | async-done | bytes 524304 | tf_op jit(solution)/shard_map/psum | solution.py:22
  521.1 2.1 fusion.13
  526.3 71.7 %all-reduce.16.cloned.1.call-done = f32[2,256,256]{2,1,0:T(8,128)} async-done(((f32[2,256,256]{2,1,0:T(8,128)}), f32[2,256,256]{2,1,0:T(8,128)}) %all-reduce.16.cloned.1.call-update) | async-done | bytes 524304 | tf_op jit(solution)/shard_map/psum | solution.py:22
  598.1 2.1 fusion.12
  603.3 2.5 copy.68
  607.4 67.7 %all-reduce.18.cloned.1.call-done = f32[2,256,256]{2,1,0:T(8,128)} async-done(((f32[2,256,256]{2,1,0:T(8,128)}), f32[2,256,256]{2,1,0:T(8,128)}) %all-reduce.18.cloned.1.call-update) | async-done | bytes 524304 | tf_op jit(solution)/shard_map/psum | solution.py:22
  675.1 2.1 fusion.11
  680.3 32.3 %all_gather.7 = f32[2,256,256]{2,0,1:T(2,128)S(1)} all-gather(f32[2,32,256]{2,0,1:T(2,128)S(1)} %copy.66), channel_id=1, replica_groups=mesh['fsdp'=8,'tp'=4] {'fsdp'}, dimensions={1}, use_global_device_ids=true | all-gather | bytes 589824 | tf_op jit(solution)/shard_map/all_gather | solution.py:60
  712.5 3.4 fusion.3
  717.3 36.1 %all-reduce.20.cloned.1.call-done = f32[2,256,256]{2,1,0:T(8,128)} async-done(((f32[2,256,256]{2,1,0:T(8,128)}), f32[2,256,256]{2,1,0:T(8,128)}) %all-reduce.20.cloned.1.call-update) | async-done | bytes 524304 | tf_op jit(solution)/shard_map/psum | solution.py:22
  753.4 2.1 fusion.10
  (40 shorter events, 18.5 us)
Async XLA Ops:
  7.2 65.2 %copy-start = (bf16[2,1024,256]{2,1,0:T(8,128)(2,1)S(1)}, bf16[2,1024,256]{2,1,0:T(8,128)(2,1)}, u32[]{:S(2)}) copy-start(bf16[2,1024,256]{2,1,0:T(8,128)(2,1)} %param.7) | copy-start | bytes 3145732
  7.2 65.2 %all-gather.2.cloned.1.call-start = ((), (), s32[]{:S(2)}) async-start(), calls=%async_computation.1 | async-start | bytes 10485760 | tf_op jit(solution)/shard_map/all_gather | solution.py:45
  11.3 220.5 %reduce-scatter.2.cloned.1.call-start = ((), (), s32[]{:S(2)}) async-start(), calls=%async_computation.2 | async-start | bytes 9437184 | tf_op jit(solution)/shard_map/reduce_scatter | solution.py:46
  82.5 149.2 %copy-start.1 = (f32[2,512,256]{2,1,0:T(8,128)S(1)}, f32[2,512,256]{2,1,0:T(8,128)}, u32[]{:S(2)}) copy-start(f32[2,512,256]{2,1,0:T(8,128)} %param.8) | copy-start | bytes 3145732
  82.6 225.0 %all-reduce.8.cloned.1.call-start = ((), (), s32[]{:S(2)}) async-start(), calls=%async_computation.3 | async-start | bytes 1048576 | tf_op jit(solution)/shard_map/psum | solution.py:52
  235.6 110.8 %all-reduce.10.cloned.1.call-start = ((), (), s32[]{:S(2)}) async-start(), calls=%async_computation.4 | async-start | bytes 2097152 | tf_op jit(solution)/shard_map/psum | solution.py:62
  311.0 131.2 %all-reduce.12.cloned.1.call-start = ((), (), s32[]{:S(2)}) async-start(), calls=%async_computation.5 | async-start | bytes 1048576 | tf_op jit(solution)/shard_map/psum | solution.py:22
  373.0 148.1 %all-reduce.14.cloned.1.call-start = ((), (), s32[]{:S(2)}) async-start(), calls=%async_computation.6 | async-start | bytes 1048576 | tf_op jit(solution)/shard_map/psum | solution.py:22
  449.3 156.6 %copy-start.2 = (f32[2,32,256]{2,1,0:T(8,128)S(1)}, f32[2,32,256]{2,1,0:T(8,128)}, u32[]{:S(2)}) copy-start(f32[2,32,256]{2,1,0:T(8,128)} %param.10) | copy-start | bytes 196612
  449.3 156.6 %copy-start.3 = (f32[2,32,256]{2,1,0:T(8,128)S(1)}, f32[2,32,256]{2,1,0:T(8,128)}, u32[]{:S(2)}) copy-start(f32[2,32,256]{2,1,0:T(8,128)} %param.11) | copy-start | bytes 196612
  449.3 148.8 %all-reduce.16.cloned.1.call-start = ((), (), s32[]{:S(2)}) async-start(), calls=%async_computation.7 | async-start | bytes 1048576 | tf_op jit(solution)/shard_map/psum | solution.py:22
  526.3 148.8 %all-reduce.18.cloned.1.call-start = ((), (), s32[]{:S(2)}) async-start(), calls=%async_computation.8 | async-start | bytes 1048576 | tf_op jit(solution)/shard_map/psum | solution.py:22
  603.3 150.1 %all-reduce.20.cloned.1.call-start = ((), (), s32[]{:S(2)}) async-start(), calls=%async_computation.9 | async-start | bytes 1048576 | tf_op jit(solution)/shard_map/psum | solution.py:22
Sparse Core Ops, SparseCore 0:
  11.4 60.9 all-gather.1
  82.7 149.0 reduce-scatter.1
  236.1 71.3 all-reduce.7
  311.1 35.3 all-reduce.9
  373.1 69.0 all-reduce.11
  449.4 71.6 all-reduce.13
  526.4 71.6 all-reduce.15
  603.4 71.6 all-reduce.17
  680.4 72.9 all-reduce.19
where the time goes:
time: 765 us; the launch traced here: 764 us
  waiting for transfers between devices  634 us (83%)
  blocking collectives  53.6 us (7%)
  matrix products  50.2 us (7%)
  between operations  14 us (2%)
  local copies, waits for them, and re-layouts  9.23 us (1%)
    psum x5, waiting for transfers between devices, gram_total(): return lax.psum(value, 'fsdp')  316 us
    reduce_scatter x1, waiting for transfers between devices, body(): lax.psum_scatter(jnp.einsum('tr,mtc->rmc', gathered, out_grads, preferred...  149 us
    psum x1, waiting for transfers between devices, body(): lax.psum(jnp.einsum('mdk,dmc->mkc', bases, grad_part, precision=high), 'f...  71.9 us
    all_gather x1, waiting for transfers between devices, body(): gathered = lax.all_gather(activations, 'tp', axis=1, tiled=True)  61.1 us
    psum x1, waiting for transfers between devices, body(): whole_cand = lax.psum(cand_part, 'tp')  35.5 us
    all_gather x1, blocking collectives, body(): step_full = lax.all_gather(adam_step, 'fsdp', axis=1, tiled=True)  32.3 us
    psum x1, blocking collectives, norm_total(): return lax.psum(value, 'fsdp')  21.3 us
  transfers between devices with their start and end apart: 9, of which 9 were waited for; matrix products, arithmetic and copies ran while one was open for 1% of the time, Pallas kernels for 0%

commit v1 on v0

v1 whole, which is shorter than its diff:
```python
import functools

import jax
import jax.numpy as jnp
from jax import lax
from jax.experimental import pallas as pl
from jax.experimental.pallas import tpu as pltpu
from jax.sharding import PartitionSpec as P

NS_STEPS = 5


COEF_A = 3.4445
COEF_B = -4.775
COEF_C = 2.0315
BETA_ONE = 0.9
BETA_TWO = 0.999
CORRECT_ONE = 1.0 - 0.9**10
CORRECT_TWO = 1.0 - 0.999**10
EPSILON = 1e-08
NORM_EPS = 1e-07
RATE = 2.0
HIGH = lax.Precision.HIGHEST
MESH = pl.DeviceIdType.MESH


def exchange_kernel(axis, count, scatter, x_ref, out_ref, own_sem, send_sem, recv_sem):
    me = lax.axis_index(axis)
    barrier = pltpu.get_barrier_semaphore()
    for hop in range(1, count):
        peer = lax.rem(me + hop, count)
        pl.semaphore_signal(barrier, inc=1, device_id={axis: peer}, device_id_type=MESH)
    own = pltpu.make_async_copy(x_ref.at[me] if scatter else x_ref, out_ref.at[me], own_sem)
    own.start()
    pl.semaphore_wait(barrier, count - 1)
    copies = []
    for hop in range(1, count):
        peer = lax.rem(me + hop, count)
        copy = pltpu.make_async_remote_copy(
            src_ref=x_ref.at[peer] if scatter else x_ref,
            dst_ref=out_ref.at[me],
            send_sem=send_sem.at[hop],
            recv_sem=recv_sem.at[hop],
            device_id={axis: peer},
            device_id_type=MESH,
        )
        copy.start()
        copies.append(copy)
    own.wait()
    for copy in copies:
        copy.wait()


def exchange(value, axis, count, scatter, ident):
    shape = value.shape if scatter else (count,) + value.shape
    return pl.pallas_call(
        functools.partial(exchange_kernel, axis, count, scatter),
        out_shape=jax.ShapeDtypeStruct(shape, value.dtype),
        in_specs=[pl.BlockSpec(memory_space=pl.ANY)],
        out_specs=pl.BlockSpec(memory_space=pl.ANY),
        scratch_shapes=[
            pltpu.SemaphoreType.DMA,
            pltpu.SemaphoreType.DMA((count,)),
            pltpu.SemaphoreType.DMA((count,)),
        ],
        compiler_params=pltpu.CompilerParams(collective_id=ident, has_side_effects=True),
    )(value)


def spread_kernel(sends, takes, x_ref, out_ref, own_sem, send_sem, recv_sem):
    me = (lax.axis_index("fsdp"), lax.axis_index("tp"))
    barrier = pltpu.get_barrier_semaphore()

    def other(where):
        return jnp.logical_or(where[0] != me[0], where[1] != me[1])

    for where in takes(me):
        pl.semaphore_signal(barrier, inc=1, device_id=where, device_id_type=MESH)
    targets = sends(me)
    pl.semaphore_wait(barrier, len(targets))

    def remote(index, where, slot):
        return pltpu.make_async_remote_copy(
            src_ref=x_ref,
            dst_ref=out_ref.at[slot],
            send_sem=send_sem.at[index],
            recv_sem=recv_sem.at[slot],
            device_id=where,
            device_id_type=MESH,
        )

    for index, (where, slot) in enumerate(targets):
        @pl.when(other(where))
        def _():
            remote(index, where, slot).start()

        @pl.when(jnp.logical_not(other(where)))
        def _():
            pltpu.make_async_copy(x_ref, out_ref.at[slot], own_sem).start()

    for slot, where in enumerate(takes(me)):
        @pl.when(other(where))
        def _():
            remote(0, where, slot).wait_recv()

        @pl.when(jnp.logical_not(other(where)))
        def _():
            pltpu.make_async_copy(x_ref, out_ref.at[slot], own_sem).wait()

    for index, (where, slot) in enumerate(targets):
        @pl.when(other(where))
        def _():
            remote(index, where, slot).wait_send()


def spread(value, sends, takes, n_sends, n_takes, ident):
    return pl.pallas_call(
        functools.partial(spread_kernel, sends, takes),
        out_shape=jax.ShapeDtypeStruct((n_takes,) + value.shape, value.dtype),
        in_specs=[pl.BlockSpec(memory_space=pl.ANY)],
        out_specs=pl.BlockSpec(memory_space=pl.ANY),
        scratch_shapes=[
            pltpu.SemaphoreType.DMA,
            pltpu.SemaphoreType.DMA((n_sends,)),
            pltpu.SemaphoreType.DMA((n_takes,)),
        ],
        compiler_params=pltpu.CompilerParams(collective_id=ident, has_side_effects=True),
    )(value)


def halves(value):
    head = lax.reduce_precision(value, 8, 7)
    return head.astype(jnp.bfloat16), (value - head).astype(jnp.bfloat16)


def mixed(form, exact, value):
    head, tail = halves(value)
    dot = functools.partial(jnp.einsum, form, preferred_element_type=jnp.float32)
    return dot(exact, head) + dot(exact, tail)


def orthogonal_mix(raw):
    rank = raw.shape[-1]
    eye = jnp.eye(rank, dtype=jnp.float32)
    scale = (jnp.sqrt(jnp.sum(raw * eye, axis=(1, 2))) + NORM_EPS)[:, None, None]
    gram = raw / scale / scale
    mul = functools.partial(jnp.einsum, "mkl,mlj->mkj", precision=HIGH)
    total = None
    for step in range(NS_STEPS):
        mixer = COEF_A * eye + COEF_B * gram + COEF_C * mul(gram, gram)
        total = mixer if total is None else mul(total, mixer)
        if step < NS_STEPS - 1:
            gram = mul(mul(mixer, gram), mixer)
    return total, scale


def body(nf, nt, activations, out_grads, bases, weights, first_moment, second_moment):
    tokens, feats = activations.shape
    mats, rows, rank = bases.shape
    slab = mats * rank // nt
    per = feats // rows
    mine_f, mine_t = lax.axis_index("fsdp"), lax.axis_index("tp")

    def base_sends(me):
        return [
            ((me[1] + nt * i, me[0] // per), lax.rem(me[0], per)) for i in range(nf // nt)
        ]

    def base_takes(me):
        return [(me[1] * per + i, lax.rem(me[0], nt)) for i in range(per)]

    own_bases = spread(bases, base_sends, base_takes, nf // nt, per, 0)
    own_bases = jnp.transpose(own_bases, (0, 2, 1, 3)).reshape(feats, mats * rank)
    outs = exchange(
        jnp.stack([out_grads[j * mats // nt] for j in range(nt)]), "tp", nt, True, 1
    )

    part = mixed("tf,fjk->jtk", activations, own_bases.reshape(feats, nt, slab))
    along = jnp.sum(exchange(part, "tp", nt, True, 2), axis=0)

    part = mixed("jtc,tk->kjc", outs, along).reshape(nf, -1, nt * outs.shape[2])
    part = jnp.sum(exchange(part, "fsdp", nf, True, 3), axis=0)
    proj = exchange(part, "fsdp", nf, False, 4).reshape(slab, nt, -1)

    rank_rows = first_moment.shape[1]
    picked = lax.dynamic_slice_in_dim(proj, lax.rem(mine_f * rank_rows, slab), rank_rows, 0)
    picked = lax.all_gather(picked, "tp")
    picked = lax.dynamic_index_in_dim(picked, mine_t, 2, False)
    spot = mine_f * rank_rows // slab
    own_proj = jnp.stack(
        [lax.dynamic_index_in_dim(picked, m * (nt // mats) + spot, 0, False) for m in range(mats)]
    )
    new_first = BETA_ONE * first_moment + (1.0 - BETA_ONE) * own_proj
    new_second = BETA_TWO * second_moment + (1.0 - BETA_TWO) * own_proj * own_proj
    adam_step = new_first / CORRECT_ONE / (jnp.sqrt(new_second / CORRECT_TWO) + EPSILON)
    step_full = lax.all_gather(adam_step, "fsdp", axis=1, tiled=True)
    new_weights = weights - RATE * jnp.einsum("mdk,mkc->mdc", bases, step_full, precision=HIGH)

    back = mixed("jtc,kjc->tk", outs, proj)
    back = exchange(back, "tp", nt, False, 5)
    part = mixed("tf,jtk->fjk", activations, back).reshape(nf, feats // nf, mats * rank)
    cand = jnp.sum(exchange(part, "fsdp", nf, True, 6), axis=0)

    def cand_sends(me):
        flat = me[1] * nf + me[0]
        return [((flat // nt, i), lax.rem(flat, nt)) for i in range(nt)]

    def cand_takes(me):
        return [
            (lax.rem(me[0] * nt + i, nf), (me[0] * nt) // nf) for i in range(nt)
        ]

    cand = spread(cand, cand_sends, cand_takes, nt, nt, 7).reshape(rows, mats, rank)

    raw = jnp.einsum("dmk,dml->mkl", cand, cand, precision=HIGH)
    raw = jnp.sum(exchange(raw.reshape(nf, -1, rank), "fsdp", nf, True, 8), axis=0)
    raw = exchange(raw, "fsdp", nf, False, 9).reshape(mats, rank, rank)
    mixer, scale = orthogonal_mix(raw)
    new_bases = jnp.einsum("dmk,mkl->mdl", cand, mixer, precision=HIGH) / scale
    return (new_weights, new_first, new_second, new_bases)


def solution(mesh):
    return jax.shard_map(
        functools.partial(body, mesh.shape["fsdp"], mesh.shape["tp"]),
        mesh=mesh,
        in_specs=(
            P("fsdp", "tp"),
            P(None, "fsdp", "tp"),
            P(None, "fsdp", None),
            P(None, "fsdp", "tp"),
            P(None, "fsdp", "tp"),
            P(None, "fsdp", "tp"),
        ),
        out_specs=(
            P(None, "fsdp", "tp"),
            P(None, "fsdp", "tp"),
            P(None, "fsdp", "tp"),
            P(None, "fsdp", None),
        ),
        check_vma=False,
    )
```

time: 765 us -> 422 us (0.55)
  waiting for transfers between devices: 634 us -> 0 us
  Pallas kernels: 0 us -> 298 us
  local copies, waits for them, and re-layouts: 9.23 us -> 26.5 us
  between operations: 14 us -> 1.1 us
  matrix products: 50.2 us -> 38.6 us
  other arithmetic: 2.99 us -> 11.5 us
    psum x7 -> x0, waiting for transfers between devices: 424 us -> none  [the longest x5 316 us: gram_total(): return lax.psum(value, 'fsdp')]
    pallas_call x0 -> x10, Pallas kernels: none -> 298 us  [the longest x8 238 us: exchange(): pl.pallas_call(functools.partial(exchange_kernel, axis, count, scatter),...]
    reduce_scatter x1 -> x0, waiting for transfers between devices: 149 us -> none  [body(): lax.psum_scatter(jnp.einsum('tr,mtc->rmc', gathered, out_grads, preferred...]
    all_gather x1 -> x0, waiting for transfers between devices: 61.1 us -> none  [body(): gathered = lax.all_gather(activations, 'tp', axis=1, tiled=True)]
    psum x1 -> x0, blocking collectives: 21.3 us -> none  [norm_total(): return lax.psum(value, 'fsdp')]
    dot_general x19 -> x28, matrix products: 50.2 us -> 38.6 us  [the longest x8 16.6 us: mixed(): return dot(exact, head) + dot(exact, tail)]
    all_gather x0 -> x1, blocking collectives: none -> 11.3 us  [body(): picked = lax.all_gather(picked, 'tp')]
    reshape x0 -> x4, local copies, waits for them, and re-layouts: none -> 8.16 us  [the longest x1 2.97 us: body(): mixed('tf,jtk->fjk', activations, back)]
  transfers between devices with their start and end apart: 9 -> 0, of which waited for: 9 -> 0; matrix products, arithmetic and copies ran while one was open for 1% -> 0% of each run, Pallas kernels for 0% -> 0%
where the time goes in v1:
time: 422 us
  Pallas kernels  298 us (71%)
  blocking collectives  46 us (11%)
  matrix products  38.6 us (9%)
  local copies, waits for them, and re-layouts  26.5 us (6%)
  other arithmetic  11.5 us (3%)
    pallas_call x8, Pallas kernels, exchange(): pl.pallas_call(functools.partial(exchange_kernel, axis, count, scatter),...  238 us
    pallas_call x2, Pallas kernels, spread(): pl.pallas_call(functools.partial(spread_kernel, sends, takes), out_shape=...  60 us
    all_gather x1, blocking collectives, body(): step_full = lax.all_gather(adam_step, 'fsdp', axis=1, tiled=True)  34.7 us
    dot_general x8, matrix products, mixed(): return dot(exact, head) + dot(exact, tail)  16.6 us
    all_gather x1, blocking collectives, body(): picked = lax.all_gather(picked, 'tp')  11.3 us

profile of v1, /device:TPU:0, one launch (start us, length us, event | category | flops | bytes accessed | tf_op | source)
XLA Modules:
  0.0 421.7 jit_solution(15116284814307365579)
XLA Ops:
  3.9 26.3 %shard_map.95 = bf16[4,1024,256]{2,1,0:T(8,128)(2,1)} custom-call(bf16[4,1024,256]{2,1,0:T(8,128)(2,1)} %pad_maximum_fusion.x_ref), custom_call_target="tpu_custom_call" | custom-call | tf_op jit(solution)/shard_map/pallas_call | solution.py:56
  30.2 35.5 %shard_map.93 = f32[2,2,512,256]{3,2,1,0:T(8,128)} custom-call(f32[2,512,256]{2,1,0:T(8,128)} %x_ref.1), custom_call_target="tpu_custom_call" | custom-call | tf_op jit(solution)/shard_map/pallas_call | solution.py:117
  65.7 4.2 copy.59
  69.9 4.1 reshape_reshape.3
  74.0 3.0 fusion.6
  77.0 2.6 add_bitcast_fusion.x_ref
  79.6 60.6 %shard_map.94 = f32[4,1024,128]{2,1,0:T(8,128)} custom-call(f32[4,1024,128]{2,1,0:T(8,128)} %add_bitcast_fusion.x_ref), custom_call_target="tpu_custom_call" | custom-call | tf_op jit(solution)/shard_map/pallas_call | solution.py:56
  146.1 13.8 %shard_map.96 = f32[8,16,1024]{2,1,0:T(8,128)} custom-call(f32[8,16,1024]{2,1,0:T(8,128)} %reshape.47.x_ref), custom_call_target="tpu_custom_call" | custom-call | tf_op jit(solution)/shard_map/pallas_call | solution.py:56
  161.7 15.9 %shard_map.97 = f32[8,16,1024]{2,1,0:T(8,128)} custom-call(f32[16,1024]{1,0:T(8,128)} %reduce_sum.53.x_ref), custom_call_target="tpu_custom_call" | custom-call | tf_op jit(solution)/shard_map/pallas_call | solution.py:56
  182.9 23.8 %shard_map.98 = f32[4,1024,128]{2,1,0:T(8,128)} custom-call(f32[1024,128]{1,0:T(8,128)} %fusion.22.x_ref), custom_call_target="tpu_custom_call" | custom-call | tf_op jit(solution)/shard_map/pallas_call | solution.py:56
  206.7 3.0 fusion.2
  212.8 3.0 copy.85.x_ref
  215.7 41.7 %shard_map.99 = f32[8,128,512]{2,1,0:T(8,128)} custom-call(f32[8,128,512]{2,1,0:T(8,128)} %copy.85.x_ref), custom_call_target="tpu_custom_call" | custom-call | tf_op jit(solution)/shard_map/pallas_call | solution.py:56
  257.4 2.5 reduce_sum.54.x_ref
  259.9 24.5 %shard_map.100 = f32[4,128,512]{2,1,0:T(8,128)} custom-call(f32[128,512]{1,0:T(8,128)} %reduce_sum.54.x_ref), custom_call_target="tpu_custom_call" | custom-call | tf_op jit(solution)/shard_map/pallas_call | solution.py:117
  284.4 2.8 reshape.50
  287.3 4.2 %fusion.25 = f32[2,256,256]{2,1,0:T(8,128)} fusion(f32[512,2,256]{2,1,0:T(2,128)} %reshape.50), kind=kOutput, calls=%fused_computation.35 | convolution fusion | flops 805306368 | bytes 1572864 | tf_op jit(solution)/shard_map/dmk,dml->mkl/dot_general | solution.py:215
  291.5 39.2 %shard_map.101 = f32[8,64,256]{2,1,0:T(8,128)} custom-call(f32[8,64,256]{2,1,0:T(8,128)} %bitcast.95), custom_call_target="tpu_custom_call" | custom-call | tf_op jit(solution)/shard_map/pallas_call | solution.py:56
  332.4 16.7 %shard_map.102 = f32[8,64,256]{2,1,0:T(8,128)} custom-call(f32[64,256]{1,0:T(8,128)} %reduce_sum.55.x_ref), custom_call_target="tpu_custom_call" | custom-call | tf_op jit(solution)/shard_map/pallas_call | solution.py:56
  364.6 11.3 %all-gather = f32[128,4,256]{2,1,0:T(4,128)} all-gather(f32[32,4,256]{2,1,0:T(4,128)S(1)} %constant_dynamic-slice_fusion.2), channel_id=2, replica_groups=mesh['fsdp'=8,'tp'=4] {'tp'}, dimensions={0}, use_global_device_ids=true | all-gather | bytes 655360 | tf_op jit(solution)/shard_map/all_gather | solution.py:187
  377.7 34.7 %all_gather.11 = f32[2,256,256]{2,1,0:T(8,128)} all-gather(f32[2,32,256]{2,1,0:T(8,128)S(1)} %get-tuple-element.20), channel_id=1, replica_groups=mesh['fsdp'=8,'tp'=4] {'fsdp'}, dimensions={1}, use_global_device_ids=true | all-gather | bytes 589824 | tf_op jit(solution)/shard_map/all_gather | solution.py:196
  412.4 2.5 copy.67
  414.9 4.2 %fusion.16 = f32[2,512,256]{1,2,0:T(8,128)} fusion(f32[2,512,256]{1,2,0:T(8,128)} %copy.67, f32[2,256,256]{2,1,0:T(8,128)} %all_gather.11, f32[2,512,256]{2,1,0:T(8,128)S(1)} %copy-done.6), kind=kOutput, calls=%fused_computation.20 | convolution fusion | flops 805830656 | bytes 3670016 | tf_op jit(solution)/shard_map/mdk,mkc->mdc/dot_general | solution.py:197
  419.1 2.5 copy.76
  (66 shorter events, 37.8 us)
Async XLA Ops:
  0.6 73.4 %copy-start = (bf16[1024,1024]{1,0:T(8,128)(2,1)S(1)}, bf16[1024,1024]{1,0:T(8,128)(2,1)}, u32[]{:S(2)}) copy-start(bf16[1024,1024]{1,0:T(8,128)(2,1)} %param.6) | copy-start | bytes 6291460
  0.6 1.7 copy-start.8
  74.0 3.0 copy-start.4
  142.0 2.2 copy-start.1
  178.9 2.5 copy-start.2
  206.7 3.0 copy-start.3
  349.2 1.6 copy-start.5
  360.5 2.0 copy-start.7
  362.5 14.4 %copy-start.9 = (f32[2,32,256]{2,1,0:T(8,128)S(1)}, f32[2,32,256]{2,1,0:T(8,128)}, u32[]{:S(2)}) copy-start(f32[2,32,256]{2,1,0:T(8,128)} %param.10) | copy-start | bytes 196612
  362.6 14.4 %copy-start.10 = (f32[2,32,256]{2,1,0:T(8,128)S(1)}, f32[2,32,256]{2,1,0:T(8,128)}, u32[]{:S(2)}) copy-start(f32[2,32,256]{2,1,0:T(8,128)} %param.11) | copy-start | bytes 196612
  364.6 50.3 %copy-start.6 = (f32[2,512,256]{2,1,0:T(8,128)S(1)}, f32[2,512,256]{2,1,0:T(8,128)}, u32[]{:S(2)}) copy-start(f32[2,512,256]{2,1,0:T(8,128)} %x_ref.1) | copy-start | bytes 3145732

commit v2 on v0

v2 whole, which is shorter than its diff:
```python
import functools

import jax
import jax.numpy as jnp
from jax import lax
from jax.experimental import pallas as pl
from jax.experimental.pallas import tpu as pltpu
from jax.sharding import PartitionSpec as P

NS_STEPS = 5


COEF_A = 3.4445
COEF_B = -4.775
COEF_C = 2.0315
BETA_ONE = 0.9
BETA_TWO = 0.999
CORRECT_ONE = 1.0 - 0.9**10
CORRECT_TWO = 1.0 - 0.999**10
EPSILON = 1e-08
NORM_EPS = 1e-07
RATE = 2.0
HIGH = lax.Precision.HIGHEST
MESH = pl.DeviceIdType.MESH


class Exchange:
    def __init__(self, axis, count, scatter):
        self.axis, self.count, self.scatter = axis, count, scatter

    def shape(self, shape):
        return shape if self.scatter else (self.count,) + shape

    def scratch(self):
        return [
            pltpu.SemaphoreType.DMA,
            pltpu.SemaphoreType.DMA((self.count,)),
            pltpu.SemaphoreType.DMA((self.count,)),
        ]

    def greet(self, barrier):
        me = lax.axis_index(self.axis)
        for hop in range(1, self.count):
            peer = lax.rem(me + hop, self.count)
            pl.semaphore_signal(
                barrier, inc=1, device_id={self.axis: peer}, device_id_type=MESH
            )
        return self.count - 1

    def start(self, x_ref, out_ref, own_sem, send_sem, recv_sem):
        me = lax.axis_index(self.axis)
        own = x_ref.at[me] if self.scatter else x_ref
        self.copies = [pltpu.make_async_copy(own, out_ref.at[me], own_sem)]
        for hop in range(1, self.count):
            peer = lax.rem(me + hop, self.count)
            self.copies.append(
                pltpu.make_async_remote_copy(
                    src_ref=x_ref.at[peer] if self.scatter else x_ref,
                    dst_ref=out_ref.at[me],
                    send_sem=send_sem.at[hop],
                    recv_sem=recv_sem.at[hop],
                    device_id={self.axis: peer},
                    device_id_type=MESH,
                )
            )
        for copy in self.copies[1:]:
            copy.start()
        self.copies[0].start()

    def finish(self, *refs):
        for copy in self.copies:
            copy.wait()


class Spread:
    def __init__(self, sends, takes, n_sends, n_takes):
        self.sends, self.takes, self.n_sends, self.n_takes = sends, takes, n_sends, n_takes

    def shape(self, shape):
        return (self.n_takes,) + shape

    def scratch(self):
        return [
            pltpu.SemaphoreType.DMA,
            pltpu.SemaphoreType.DMA((self.n_sends,)),
            pltpu.SemaphoreType.DMA((self.n_takes,)),
        ]

    def greet(self, barrier):
        for where in self.takes((lax.axis_index("fsdp"), lax.axis_index("tp"))):
            pl.semaphore_signal(barrier, inc=1, device_id=where, device_id_type=MESH)
        return self.n_sends

    def each(self, pairs, remote, local):
        me = (lax.axis_index("fsdp"), lax.axis_index("tp"))
        for index, (where, slot) in enumerate(pairs(me)):
            other = jnp.logical_or(where[0] != me[0], where[1] != me[1])

            @pl.when(other)
            def _():
                remote(index, where, slot)

            if local is not None:

                @pl.when(jnp.logical_not(other))
                def _():
                    local(slot)

    def start(self, x_ref, out_ref, own_sem, send_sem, recv_sem):
        def copy(index, where, slot):
            return pltpu.make_async_remote_copy(
                src_ref=x_ref,
                dst_ref=out_ref.at[slot],
                send_sem=send_sem.at[index],
                recv_sem=recv_sem.at[slot],
                device_id=where,
                device_id_type=MESH,
            )

        self.copy = copy
        self.each(
            self.sends,
            lambda *at: copy(*at).start(),
            lambda slot: pltpu.make_async_copy(x_ref, out_ref.at[slot], own_sem).start(),
        )

    def finish(self, x_ref, out_ref, own_sem, send_sem, recv_sem):
        self.each(
            lambda me: [(where, slot) for slot, where in enumerate(self.takes(me))],
            lambda index, where, slot: self.copy(0, where, slot).wait_recv(),
            lambda slot: pltpu.make_async_copy(x_ref, out_ref.at[slot], own_sem).wait(),
        )
        self.each(self.sends, lambda *at: self.copy(*at).wait_send(), None)


class Chain:
    def __init__(self, count, per, parts):
        self.count, self.per, self.parts = count, per, parts

    def shape(self, shape):
        return shape[:1] + (self.per,) + shape[1:]

    def scratch(self):
        pieces = self.pieces
        return [
            pltpu.SemaphoreType.DMA((pieces,)),
            pltpu.SemaphoreType.DMA((2, pieces)),
            pltpu.SemaphoreType.DMA((pieces,)),
            pltpu.SemaphoreType.DMA((self.per, pieces)),
            pltpu.SemaphoreType.DMA((self.per, pieces)),
        ]

    @property
    def pieces(self):
        return 2 * self.parts

    def places(self):
        me = lax.axis_index("fsdp")
        return me // self.per, lax.rem(me, self.per)

    def mates(self):
        group, spot = self.places()
        return [
            {"fsdp": group * self.per + lax.rem(spot + hop, self.per)}
            for hop in range(1, self.per)
        ]

    def beside(self, step):
        group, spot = self.places()
        return {"fsdp": lax.rem(group + step + self.count, self.count) * self.per + spot}

    def greet(self, barrier):
        for where in self.mates() + [self.beside(1), self.beside(-1)]:
            pl.semaphore_signal(barrier, inc=1, device_id=where, device_id_type=MESH)
        return self.per + 1

    def start(self, x_ref, out_ref, own_sem, pass_sem, come_sem, swap_sem, meet_sem):
        group, spot = self.places()
        source = lax.axis_index("tp")
        size = x_ref.shape[1] // self.parts

        def at(piece, owner):
            mat, part = piece // self.parts, piece % self.parts
            return out_ref.at[mat, owner, pl.ds(part * size, size)]

        def own(piece):
            mat, part = piece // self.parts, piece % self.parts
            return pltpu.make_async_copy(
                x_ref.at[mat, pl.ds(part * size, size)], at(piece, spot), own_sem.at[piece]
            )

        def along(piece, way):
            return pltpu.make_async_remote_copy(
                src_ref=at(piece, spot),
                dst_ref=at(piece, spot),
                send_sem=pass_sem.at[way, piece],
                recv_sem=come_sem.at[piece],
                device_id=self.beside(1 if way == 0 else -1),
                device_id_type=MESH,
            )

        def swap(piece, hop):
            return pltpu.make_async_remote_copy(
                src_ref=at(piece, spot),
                dst_ref=at(piece, spot),
                send_sem=swap_sem.at[hop, piece],
                recv_sem=meet_sem.at[hop, piece],
                device_id=self.mates()[hop - 1],
                device_id_type=MESH,
            )

        onward = (
            jnp.logical_and(group >= source, group < self.count - 1),
            jnp.logical_and(group <= source, group > 0),
        )

        @pl.when(group == source)
        def _():
            for piece in range(self.pieces):
                own(piece).start()

        for piece in range(self.pieces):

            @pl.when(group == source)
            def _():
                own(piece).wait()

            @pl.when(group != source)
            def _():
                along(piece, 0).wait_recv()

            for way in range(2):

                @pl.when(onward[way])
                def _():
                    along(piece, way).start()

            for hop in range(1, self.per):
                swap(piece, hop).start()

        for piece in range(self.pieces):
            for hop in range(1, self.per):
                swap(piece, hop).wait()
            for way in range(2):

                @pl.when(onward[way])
                def _():
                    along(piece, way).wait_send()

    def finish(self, *refs):
        pass


def transfer_kernel(moves, *refs):
    count = len(moves)
    sems, spans = list(refs[2 * count :]), []
    for index, move in enumerate(moves):
        held = len(move.scratch())
        spans.append((refs[index], refs[count + index], *sems[:held]))
        sems = sems[held:]
    barrier = pltpu.get_barrier_semaphore()
    pl.semaphore_wait(barrier, sum(move.greet(barrier) for move in moves))
    for move, span in zip(moves, spans):
        move.start(*span)
    for move, span in zip(moves, spans):
        move.finish(*span)


def transfer(ident, *pairs):
    values, moves = [pair[0] for pair in pairs], [pair[1] for pair in pairs]
    results = pl.pallas_call(
        functools.partial(transfer_kernel, moves),
        out_shape=[
            jax.ShapeDtypeStruct(move.shape(value.shape), value.dtype)
            for value, move in zip(values, moves)
        ],
        in_specs=[pl.BlockSpec(memory_space=pl.ANY)] * len(values),
        out_specs=[pl.BlockSpec(memory_space=pl.ANY)] * len(values),
        scratch_shapes=[sem for move in moves for sem in move.scratch()],
        compiler_params=pltpu.CompilerParams(collective_id=ident, has_side_effects=True),
    )(*values)
    return results[0] if len(results) == 1 else results


def halves(value):
    head = lax.reduce_precision(value, 8, 7)
    return head.astype(jnp.bfloat16), (value - head).astype(jnp.bfloat16)


def mixed(form, exact, value):
    head, tail = halves(value)
    dot = functools.partial(jnp.einsum, form, preferred_element_type=jnp.float32)
    return dot(exact, head) + dot(exact, tail)


def orthogonal_mix(raw):
    rank = raw.shape[-1]
    eye = jnp.eye(rank, dtype=jnp.float32)
    scale = (jnp.sqrt(jnp.sum(raw * eye, axis=(1, 2))) + NORM_EPS)[:, None, None]
    gram = raw / scale / scale
    mul = functools.partial(jnp.einsum, "mkl,mlj->mkj", precision=HIGH)
    total = None
    for step in range(NS_STEPS):
        mixer = COEF_A * eye + COEF_B * gram + COEF_C * mul(gram, gram)
        total = mixer if total is None else mul(total, mixer)
        if step < NS_STEPS - 1:
            gram = mul(mul(mixer, gram), mixer)
    return total, scale


def body(nf, nt, activations, out_grads, bases, weights, first_moment, second_moment):
    tokens, feats = activations.shape
    mats, rows, rank = bases.shape
    slab = mats * rank // nt
    per = feats // rows
    mine_f, mine_t = lax.axis_index("fsdp"), lax.axis_index("tp")

    outs, own_bases = transfer(
        0,
        (jnp.stack([out_grads[j * mats // nt] for j in range(nt)]), Exchange("tp", nt, True)),
        (bases, Chain(nf // per, per, 2)),
    )
    own_bases = own_bases.reshape(mats, feats, rank)

    part = mixed("tf,mfk->mtk", activations, own_bases)
    part = part.reshape(mats, tokens, nt // mats, slab)
    part = jnp.transpose(part, (0, 2, 1, 3)).reshape(nt, tokens, slab)
    along = jnp.sum(transfer(1, (part, Exchange("tp", nt, True))), axis=0)

    part = mixed("jtc,tk->kjc", outs, along).reshape(nf, -1, nt * outs.shape[2])
    part = jnp.sum(transfer(2, (part, Exchange("fsdp", nf, True))), axis=0)
    proj = transfer(3, (part, Exchange("fsdp", nf, False))).reshape(slab, nt, -1)

    rank_rows = first_moment.shape[1]
    picked = lax.dynamic_slice_in_dim(proj, lax.rem(mine_f * rank_rows, slab), rank_rows, 0)
    back = mixed("jtc,kjc->tk", outs, proj)
    back, picked = transfer(
        4,
        (back, Exchange("tp", nt, False)),
        (jnp.transpose(picked, (1, 0, 2)), Exchange("tp", nt, True)),
    )

    spot = mine_f * rank_rows // slab
    own_proj = jnp.stack(
        [lax.dynamic_index_in_dim(picked, m * (nt // mats) + spot, 0, False) for m in range(mats)]
    )
    new_first = BETA_ONE * first_moment + (1.0 - BETA_ONE) * own_proj
    new_second = BETA_TWO * second_moment + (1.0 - BETA_TWO) * own_proj * own_proj
    adam_step = new_first / CORRECT_ONE / (jnp.sqrt(new_second / CORRECT_TWO) + EPSILON)

    part = mixed("tf,jtk->fjk", activations, back).reshape(nf, feats // nf, mats * rank)
    cand, step_full = transfer(
        5,
        (part, Exchange("fsdp", nf, True)),
        (adam_step, Exchange("fsdp", nf, False)),
    )
    cand = jnp.sum(cand, axis=0)
    step_full = jnp.transpose(step_full, (1, 0, 2, 3)).reshape(mats, rank, -1)
    new_weights = weights - RATE * jnp.einsum("mdk,mkc->mdc", bases, step_full, precision=HIGH)

    def cand_sends(me):
        flat = me[1] * nf + me[0]
        return [((flat // nt, i), lax.rem(flat, nt)) for i in range(nt)]

    def cand_takes(me):
        return [
            (lax.rem(me[0] * nt + i, nf), (me[0] * nt) // nf) for i in range(nt)
        ]

    raw = cand.reshape(-1, mats, rank)
    raw = jnp.einsum("dmk,dml->mkl", raw, raw, precision=HIGH).reshape(nf, -1, rank)
    raw, cand = transfer(
        6,
        (raw, Exchange("fsdp", nf, True)),
        (cand, Spread(cand_sends, cand_takes, nt, nt)),
    )
    cand = cand.reshape(rows, mats, rank)
    raw = jnp.sum(raw, axis=0)
    raw = jnp.sum(transfer(7, (raw, Exchange("tp", nt, False))), axis=0)
    raw = transfer(8, (raw, Exchange("fsdp", nf, False))).reshape(mats, rank, rank)
    mixer, scale = orthogonal_mix(raw)
    new_bases = jnp.einsum("dmk,mkl->mdl", cand, mixer, precision=HIGH) / scale
    return (new_weights, new_first, new_second, new_bases)


def solution(mesh):
    return jax.shard_map(
        functools.partial(body, mesh.shape["fsdp"], mesh.shape["tp"]),
        mesh=mesh,
        in_specs=(
            P("fsdp", "tp"),
            P(None, "fsdp", "tp"),
            P(None, "fsdp", None),
            P(None, "fsdp", "tp"),
            P(None, "fsdp", "tp"),
            P(None, "fsdp", "tp"),
        ),
        out_specs=(
            P(None, "fsdp", "tp"),
            P(None, "fsdp", "tp"),
            P(None, "fsdp", "tp"),
            P(None, "fsdp", None),
        ),
        check_vma=False,
    )
```

time: 765 us -> 381 us (0.50)
  waiting for transfers between devices: 634 us -> 0 us
  Pallas kernels: 0 us -> 302 us
  blocking collectives: 53.6 us -> 0 us
  local copies, waits for them, and re-layouts: 9.23 us -> 24.4 us
  matrix products: 50.2 us -> 36.6 us
  between operations: 14 us -> 1.11 us
  other arithmetic: 2.99 us -> 13.9 us
    psum x7 -> x0, waiting for transfers between devices: 424 us -> none  [the longest x5 316 us: gram_total(): return lax.psum(value, 'fsdp')]
    pallas_call x0 -> x9, Pallas kernels: none -> 302 us  [transfer(): pl.pallas_call(functools.partial(transfer_kernel, moves), out_shape=[jax....]
    reduce_scatter x1 -> x0, waiting for transfers between devices: 149 us -> none  [body(): lax.psum_scatter(jnp.einsum('tr,mtc->rmc', gathered, out_grads, preferred...]
    all_gather x1 -> x0, waiting for transfers between devices: 61.1 us -> none  [body(): gathered = lax.all_gather(activations, 'tp', axis=1, tiled=True)]
    all_gather x1 -> x0, blocking collectives: 32.3 us -> none  [body(): step_full = lax.all_gather(adam_step, 'fsdp', axis=1, tiled=True)]
    psum x1 -> x0, blocking collectives: 21.3 us -> none  [norm_total(): return lax.psum(value, 'fsdp')]
    dot_general x19 -> x28, matrix products: 50.2 us -> 36.6 us  [the longest x8 15.2 us: mixed(): return dot(exact, head) + dot(exact, tail)]
    reshape x0 -> x6, local copies, waits for them, and re-layouts: none -> 9.96 us  [the longest x1 2.97 us: body(): mixed('tf,jtk->fjk', activations, back)]
  transfers between devices with their start and end apart: 9 -> 0, of which waited for: 9 -> 0; matrix products, arithmetic and copies ran while one was open for 1% -> 0% of each run, Pallas kernels for 0% -> 0%
where the time goes in v2:
time: 381 us; the launch traced here: 378 us
  Pallas kernels  302 us (79%)
  matrix products  36.6 us (10%)
  local copies, waits for them, and re-layouts  24.4 us (6%)
  other arithmetic  13.9 us (4%)
    pallas_call x9, Pallas kernels, transfer(): pl.pallas_call(functools.partial(transfer_kernel, moves), out_shape=[jax....  302 us
    dot_general x8, matrix products, mixed(): return dot(exact, head) + dot(exact, tail)  15.2 us

profile of v2, /device:TPU:0, one launch (start us, length us, event | category | flops | bytes accessed | tf_op | source)
XLA Modules:
  0.0 378.2 jit_solution(7980372379573110934)
XLA Ops:
  3.9 60.4 %shard_map.93 = (bf16[4,1024,256]{2,1,0:T(8,128)(2,1)}, f32[2,2,512,256]{3,2,1,0:T(8,128)}) custom-call(bf16[4,1024,256]{2,1,0:T(8,128)(2,1)} %pad_maximum_fusion.refs_0_, f32[2,512,256]{2,1,0:T(8,128)} %refs_1_.1), custom_call_target="tpu_custom_call" | custom-call | tf_op jit(solution)/shard_map/pallas_call | solution.py:271
  64.3 2.9 copy.58
  67.2 3.0 fusion.6
  73.3 2.9 copy.60
  76.2 37.7 %shard_map.94 = f32[4,1024,128]{2,1,0:T(8,128)} custom-call(f32[4,1024,128]{2,1,0:T(8,128)} %bitcast.93), custom_call_target="tpu_custom_call" | custom-call | tf_op jit(solution)/shard_map/pallas_call | solution.py:271
  113.9 1.8 reduce_sum.61
  115.6 2.2 fusion.32
  119.8 16.9 %shard_map.95 = f32[8,16,1024]{2,1,0:T(8,128)} custom-call(f32[8,16,1024]{2,1,0:T(8,128)} %reshape.60.refs_0_), custom_call_target="tpu_custom_call" | custom-call | tf_op jit(solution)/shard_map/pallas_call | solution.py:271
  138.4 15.9 %shard_map.96 = f32[8,16,1024]{2,1,0:T(8,128)} custom-call(f32[16,1024]{1,0:T(8,128)} %reduce_sum.62.refs_0_), custom_call_target="tpu_custom_call" | custom-call | tf_op jit(solution)/shard_map/pallas_call | solution.py:271
  156.3 2.3 convolution_bitcast_fusion
  160.2 27.1 %shard_map.97 = (f32[4,1024,128]{2,1,0:T(8,128)}, f32[4,32,256]{2,1,0:T(8,128)}) custom-call(f32[1024,128]{1,0:T(8,128)} %fusion.22.refs_0_, f32[4,32,256]{2,1,0:T(8,128)} %dynamic-slice_bitcast_fusion.refs_1_), custom_call_target="tpu_custom_call" | custom-call | tf_op jit(solution)/shard_map/pallas_call | solution.py:271
  188.8 3.0 fusion.2
  193.1 1.8 copy.86
  194.9 3.0 copy.84.refs_0_
  197.9 61.3 %shard_map.98 = (f32[8,128,512]{2,1,0:T(8,128)}, f32[8,2,32,256]{3,2,1,0:T(8,128)}) custom-call(f32[8,128,512]{2,1,0:T(8,128)} %copy.84.refs_0_, f32[2,32,256]{2,1,0:T(8,128)} %get-tuple-element.36.refs_1_), custom_call_target="tpu_custom_call" | custom-call | tf_op jit(solution)/shard_map/pallas_call | solution.py:271
  259.2 1.8 reduce_sum.63.refs_1_
  262.4 19.9 %shard_map.99 = (f32[8,64,256]{2,1,0:T(8,128)}, f32[4,128,512]{2,1,0:T(8,128)}) custom-call(f32[8,64,256]{2,1,0:T(8,128)} %bitcast.99, f32[128,512]{1,0:T(8,128)} %copy-done.8), custom_call_target="tpu_custom_call" | custom-call | tf_op jit(solution)/shard_map/pallas_call | solution.py:271
  282.3 1.7 reduce_sum.64.refs_0_
  284.1 23.0 %shard_map.100 = f32[4,64,256]{2,1,0:T(8,128)} custom-call(f32[64,256]{1,0:T(8,128)} %reduce_sum.64.refs_0_), custom_call_target="tpu_custom_call" | custom-call | tf_op jit(solution)/shard_map/pallas_call | solution.py:271
  308.6 40.2 %shard_map.101 = f32[8,64,256]{2,1,0:T(8,128)} custom-call(f32[64,256]{1,0:T(8,128)} %reduce_sum.65.refs_0_), custom_call_target="tpu_custom_call" | custom-call | tf_op jit(solution)/shard_map/pallas_call | solution.py:271
  364.6 3.5 convolution_divide_fusion
  369.0 2.5 copy.72
  371.5 4.2 %fusion.16 = f32[2,512,256]{1,2,0:T(8,128)} fusion(f32[2,512,256]{1,2,0:T(8,128)} %copy.72, f32[2,256,256]{2,1,0:T(8,128)} %bitcast.98, f32[2,512,256]{2,1,0:T(8,128)S(1)} %copy-done.6), kind=kOutput, calls=%fused_computation.21 | convolution fusion | flops 805830656 | bytes 3670016 | tf_op jit(solution)/shard_map/mdk,mkc->mdc/dot_general | solution.py:359
  375.7 2.5 copy.76
  (71 shorter events, 35.7 us)
Async XLA Ops:
  0.6 66.6 %copy-start = (bf16[1024,1024]{1,0:T(8,128)(2,1)S(1)}, bf16[1024,1024]{1,0:T(8,128)(2,1)}, u32[]{:S(2)}) copy-start(bf16[1024,1024]{1,0:T(8,128)(2,1)} %param.6) | copy-start | bytes 6291460
  0.6 1.7 copy-start.7
  67.2 3.0 copy-start.4
  115.6 2.2 copy-start.1
  155.5 3.1 copy-start.2
  158.6 29.4 %copy-start.11 = (f32[2,32,256]{2,1,0:T(8,128)S(1)}, f32[2,32,256]{2,1,0:T(8,128)}, u32[]{:S(2)}) copy-start(f32[2,32,256]{2,1,0:T(8,128)} %param.10) | copy-start | bytes 196612
  158.7 29.4 %copy-start.12 = (f32[2,32,256]{2,1,0:T(8,128)S(1)}, f32[2,32,256]{2,1,0:T(8,128)}, u32[]{:S(2)}) copy-start(f32[2,32,256]{2,1,0:T(8,128)} %param.11) | copy-start | bytes 196612
  188.8 3.0 copy-start.3
  261.0 1.4 copy-start.8
  348.8 1.6 copy-start.5
  360.0 3.0 copy-start.9
  364.6 3.5 copy-start.10
  368.1 3.4 copy-start.6

commit v3 on v2

--- a/solution.py
+++ b/solution.py
@@ -318,7 +318,7 @@
     outs, own_bases = transfer(
         0,
         (jnp.stack([out_grads[j * mats // nt] for j in range(nt)]), Exchange("tp", nt, True)),
-        (bases, Chain(nf // per, per, 2)),
+        (bases, Chain(nf // per, per, 8)),
     )
     own_bases = own_bases.reshape(mats, feats, rank)
 
@@ -360,23 +360,25 @@
 
     def cand_sends(me):
         flat = me[1] * nf + me[0]
-        return [((flat // nt, i), lax.rem(flat, nt)) for i in range(nt)]
+        return [((flat // nt, lax.rem(flat, nt)), 0)]
 
     def cand_takes(me):
-        return [
-            (lax.rem(me[0] * nt + i, nf), (me[0] * nt) // nf) for i in range(nt)
-        ]
+        flat = me[0] * nt + me[1]
+        return [(lax.rem(flat, nf), flat // nf)]
 
     raw = cand.reshape(-1, mats, rank)
     raw = jnp.einsum("dmk,dml->mkl", raw, raw, precision=HIGH).reshape(nf, -1, rank)
     raw, cand = transfer(
         6,
         (raw, Exchange("fsdp", nf, True)),
-        (cand, Spread(cand_sends, cand_takes, nt, nt)),
+        (cand, Spread(cand_sends, cand_takes, 1, 1)),
+    )
+    raw = jnp.sum(raw, axis=0)
+    raw, cand = transfer(
+        7, (raw, Exchange("tp", nt, False)), (cand[0], Exchange("tp", nt, False))
     )
     cand = cand.reshape(rows, mats, rank)
     raw = jnp.sum(raw, axis=0)
-    raw = jnp.sum(transfer(7, (raw, Exchange("tp", nt, False))), axis=0)
     raw = transfer(8, (raw, Exchange("fsdp", nf, False))).reshape(mats, rank, rank)
     mixer, scale = orthogonal_mix(raw)
     new_bases = jnp.einsum("dmk,mkl->mdl", cand, mixer, precision=HIGH) / scale

time: 381 us -> 347 us (0.911)
  Pallas kernels: 302 us -> 268 us
    pallas_call x9, Pallas kernels: 302 us -> 268 us  [transfer(): pl.pallas_call(functools.partial(transfer_kernel, moves), out_shape=[jax....]
where the time goes in v3:
time: 347 us; the launch traced here: 343 us
  Pallas kernels  268 us (77%)
  matrix products  36.6 us (11%)
  local copies, waits for them, and re-layouts  24.4 us (7%)
  other arithmetic  13.9 us (4%)
    pallas_call x9, Pallas kernels, transfer(): pl.pallas_call(functools.partial(transfer_kernel, moves), out_shape=[jax....  268 us
    dot_general x8, matrix products, mixed(): return dot(exact, head) + dot(exact, tail)  15.2 us
    unnamed x29, local copies, waits for them, and re-layouts  7.12 us

profile of v3, /device:TPU:0, one launch (start us, length us, event | category | flops | bytes accessed | tf_op | source)
XLA Modules:
  0.0 343.5 jit_solution(8686797965190765057)
XLA Ops:
  3.9 59.3 %shard_map.93 = (bf16[4,1024,256]{2,1,0:T(8,128)(2,1)}, f32[2,2,512,256]{3,2,1,0:T(8,128)}) custom-call(bf16[4,1024,256]{2,1,0:T(8,128)(2,1)} %pad_maximum_fusion.refs_0_, f32[2,512,256]{2,1,0:T(8,128)} %refs_1_.1), custom_call_target="tpu_custom_call" | custom-call | tf_op jit(solution)/shard_map/pallas_call | solution.py:271
  63.2 2.9 copy.58
  66.1 3.0 fusion.6
  72.2 2.9 copy.60
  75.1 32.5 %shard_map.94 = f32[4,1024,128]{2,1,0:T(8,128)} custom-call(f32[4,1024,128]{2,1,0:T(8,128)} %bitcast.94), custom_call_target="tpu_custom_call" | custom-call | tf_op jit(solution)/shard_map/pallas_call | solution.py:271
  107.6 1.8 reduce_sum.61
  109.4 2.2 fusion.32
  113.5 14.1 %shard_map.95 = f32[8,16,1024]{2,1,0:T(8,128)} custom-call(f32[8,16,1024]{2,1,0:T(8,128)} %reshape.60.refs_0_), custom_call_target="tpu_custom_call" | custom-call | tf_op jit(solution)/shard_map/pallas_call | solution.py:271
  129.3 15.5 %shard_map.96 = f32[8,16,1024]{2,1,0:T(8,128)} custom-call(f32[16,1024]{1,0:T(8,128)} %reduce_sum.62.refs_0_), custom_call_target="tpu_custom_call" | custom-call | tf_op jit(solution)/shard_map/pallas_call | solution.py:271
  147.0 2.3 convolution_bitcast_fusion
  150.8 27.1 %shard_map.97 = (f32[4,1024,128]{2,1,0:T(8,128)}, f32[4,32,256]{2,1,0:T(8,128)}) custom-call(f32[1024,128]{1,0:T(8,128)} %fusion.22.refs_0_, f32[4,32,256]{2,1,0:T(8,128)} %dynamic-slice_bitcast_fusion.refs_1_), custom_call_target="tpu_custom_call" | custom-call | tf_op jit(solution)/shard_map/pallas_call | solution.py:271
  179.4 3.0 fusion.2
  183.7 1.8 copy.86
  185.5 3.0 copy.84.refs_0_
  188.5 61.3 %shard_map.98 = (f32[8,128,512]{2,1,0:T(8,128)}, f32[8,2,32,256]{3,2,1,0:T(8,128)}) custom-call(f32[8,128,512]{2,1,0:T(8,128)} %copy.84.refs_0_, f32[2,32,256]{2,1,0:T(8,128)} %get-tuple-element.40.refs_1_), custom_call_target="tpu_custom_call" | custom-call | tf_op jit(solution)/shard_map/pallas_call | solution.py:271
  249.8 1.8 reduce_sum.63.refs_1_
  253.0 18.4 %shard_map.99 = (f32[8,64,256]{2,1,0:T(8,128)}, f32[1,128,512]{2,1,0:T(8,128)}) custom-call(f32[8,64,256]{2,1,0:T(8,128)} %bitcast.100, f32[128,512]{1,0:T(8,128)} %copy-done.8), custom_call_target="tpu_custom_call" | custom-call | tf_op jit(solution)/shard_map/pallas_call | solution.py:271
  271.4 1.7 reduce_sum.64.refs_0_
  273.1 18.9 %shard_map.100 = (f32[4,64,256]{2,1,0:T(8,128)}, f32[4,128,512]{2,1,0:T(8,128)}) custom-call(f32[64,256]{1,0:T(8,128)} %reduce_sum.64.refs_0_, f32[128,512]{1,0:T(8,128)} %bitcast.104), custom_call_target="tpu_custom_call" | custom-call | tf_op jit(solution)/shard_map/pallas_call | solution.py:271
  293.7 20.4 %shard_map.101 = f32[8,64,256]{2,1,0:T(8,128)} custom-call(f32[64,256]{1,0:T(8,128)} %reduce_sum.65.refs_0_), custom_call_target="tpu_custom_call" | custom-call | tf_op jit(solution)/shard_map/pallas_call | solution.py:271
  329.9 3.5 %convolution_divide_fusion = f32[2,512,256]{2,1,0:T(8,128)} fusion(f32[2,256,256]{2,1,0:T(8,128)} %fusion.57, f32[512,2,256]{2,1,0:T(2,128)} %reshape.66, f32[2]{0:T(128)S(1)} %get-tuple-element.49), kind=kOutput, calls=%fused_computation.18 | convolution fusion | flops 805568512 | bytes 2621448 | tf_op jit(solution)/shard_map/dmk,mkl->mdl/dot_general | solution.py:384
  334.2 2.5 copy.72
  336.7 4.2 %fusion.16 = f32[2,512,256]{1,2,0:T(8,128)} fusion(f32[2,512,256]{1,2,0:T(8,128)} %copy.72, f32[2,256,256]{2,1,0:T(8,128)} %bitcast.99, f32[2,512,256]{2,1,0:T(8,128)S(1)} %copy-done.6), kind=kOutput, calls=%fused_computation.21 | convolution fusion | flops 805830656 | bytes 3670016 | tf_op jit(solution)/shard_map/mdk,mkc->mdc/dot_general | solution.py:359
  340.9 2.5 copy.76
  (71 shorter events, 35.7 us)
Async XLA Ops:
  0.6 65.5 %copy-start = (bf16[1024,1024]{1,0:T(8,128)(2,1)S(1)}, bf16[1024,1024]{1,0:T(8,128)(2,1)}, u32[]{:S(2)}) copy-start(bf16[1024,1024]{1,0:T(8,128)(2,1)} %param.6) | copy-start | bytes 6291460
  0.6 1.7 copy-start.7
  66.1 3.0 copy-start.4
  109.4 2.2 copy-start.1
  146.2 3.1 copy-start.2
  149.3 29.4 %copy-start.11 = (f32[2,32,256]{2,1,0:T(8,128)S(1)}, f32[2,32,256]{2,1,0:T(8,128)}, u32[]{:S(2)}) copy-start(f32[2,32,256]{2,1,0:T(8,128)} %param.10) | copy-start | bytes 196612
  149.3 29.4 %copy-start.12 = (f32[2,32,256]{2,1,0:T(8,128)S(1)}, f32[2,32,256]{2,1,0:T(8,128)}, u32[]{:S(2)}) copy-start(f32[2,32,256]{2,1,0:T(8,128)} %param.11) | copy-start | bytes 196612
  179.4 3.0 copy-start.3
  251.6 1.4 copy-start.8
  314.1 1.6 copy-start.5
  325.2 3.0 copy-start.9
  329.9 3.5 %copy-start.10 = (f32[8,2,32,256]{3,2,1,0:T(8,128)S(1)}, f32[8,2,32,256]{3,2,1,0:T(8,128)}, u32[]{:S(2)}) copy-start(f32[8,2,32,256]{3,2,1,0:T(8,128)} %get-tuple-element.18) | copy-start | bytes 1572868
  333.3 3.4 copy-start.6

commit v4 on v3

--- a/solution.py
+++ b/solution.py
@@ -25,8 +25,15 @@
 
 
 class Exchange:
-    def __init__(self, axis, count, scatter):
-        self.axis, self.count, self.scatter = axis, count, scatter
+    def __init__(self, axis, count, scatter, stride=1):
+        self.axis, self.count, self.scatter, self.stride = axis, count, scatter, stride
+
+    def place(self):
+        return lax.rem(lax.axis_index(self.axis) // self.stride, self.count)
+
+    def where(self, peer):
+        index = lax.axis_index(self.axis)
+        return {self.axis: index + (peer - self.place()) * self.stride}
 
     def shape(self, shape):
         return shape if self.scatter else (self.count,) + shape
@@ -39,16 +46,16 @@
         ]
 
     def greet(self, barrier):
-        me = lax.axis_index(self.axis)
+        me = self.place()
         for hop in range(1, self.count):
             peer = lax.rem(me + hop, self.count)
             pl.semaphore_signal(
-                barrier, inc=1, device_id={self.axis: peer}, device_id_type=MESH
+                barrier, inc=1, device_id=self.where(peer), device_id_type=MESH
             )
         return self.count - 1
 
     def start(self, x_ref, out_ref, own_sem, send_sem, recv_sem):
-        me = lax.axis_index(self.axis)
+        me = self.place()
         own = x_ref.at[me] if self.scatter else x_ref
         self.copies = [pltpu.make_async_copy(own, out_ref.at[me], own_sem)]
         for hop in range(1, self.count):
@@ -59,7 +66,7 @@
                     dst_ref=out_ref.at[me],
                     send_sem=send_sem.at[hop],
                     recv_sem=recv_sem.at[hop],
-                    device_id={self.axis: peer},
+                    device_id=self.where(peer),
                     device_id_type=MESH,
                 )
             )
@@ -348,15 +355,20 @@
     new_second = BETA_TWO * second_moment + (1.0 - BETA_TWO) * own_proj * own_proj
     adam_step = new_first / CORRECT_ONE / (jnp.sqrt(new_second / CORRECT_TWO) + EPSILON)
 
-    part = mixed("tf,jtk->fjk", activations, back).reshape(nf, feats // nf, mats * rank)
-    cand, step_full = transfer(
+    groups = nf // per
+    part = mixed("tf,jtk->fjk", activations, back).reshape(groups, per, -1, mats * rank)
+    upper = part.shape[2] * 11 // 16 // 8 * 8
+    near, far = transfer(
         5,
-        (part, Exchange("fsdp", nf, True)),
-        (adam_step, Exchange("fsdp", nf, False)),
-    )
-    cand = jnp.sum(cand, axis=0)
-    step_full = jnp.transpose(step_full, (1, 0, 2, 3)).reshape(mats, rank, -1)
-    new_weights = weights - RATE * jnp.einsum("mdk,mkc->mdc", bases, step_full, precision=HIGH)
+        (jnp.swapaxes(part[:, :, :upper], 0, 1), Exchange("fsdp", per, True)),
+        (part[:, :, upper:], Exchange("fsdp", groups, True, per)),
+    )
+    near, far = transfer(
+        9,
+        (jnp.sum(near, axis=0), Exchange("fsdp", groups, True, per)),
+        (jnp.sum(far, axis=0), Exchange("fsdp", per, True)),
+    )
+    cand = jnp.concatenate([jnp.sum(near, axis=0), jnp.sum(far, axis=0)])
 
     def cand_sends(me):
         flat = me[1] * nf + me[0]
@@ -374,9 +386,14 @@
         (cand, Spread(cand_sends, cand_takes, 1, 1)),
     )
     raw = jnp.sum(raw, axis=0)
-    raw, cand = transfer(
-        7, (raw, Exchange("tp", nt, False)), (cand[0], Exchange("tp", nt, False))
-    )
+    raw, cand, step_full = transfer(
+        7,
+        (raw, Exchange("tp", nt, False)),
+        (cand[0], Exchange("tp", nt, False)),
+        (adam_step, Exchange("fsdp", nf, False)),
+    )
+    step_full = jnp.transpose(step_full, (1, 0, 2, 3)).reshape(mats, rank, -1)
+    new_weights = weights - RATE * jnp.einsum("mdk,mkc->mdc", bases, step_full, precision=HIGH)
     cand = cand.reshape(rows, mats, rank)
     raw = jnp.sum(raw, axis=0)
     raw = transfer(8, (raw, Exchange("fsdp", nf, False))).reshape(mats, rank, rank)

time: 347 us -> 346 us (level)
  Pallas kernels: 268 us -> 257 us
  local copies, waits for them, and re-layouts: 24.4 us -> 31.9 us
    pallas_call x9 -> x10, Pallas kernels: 268 us -> 257 us  [transfer(): pl.pallas_call(functools.partial(transfer_kernel, moves), out_shape=[jax....]
    slice x0 -> x1, local copies, waits for them, and re-layouts: none -> 3.58 us  [body(): part[:, :, upper:]]
    reduce_sum x1 -> x4, other arithmetic: 1.82 us -> 5.3 us  [the longest x1 2.47 us: body(): jnp.sum(near, axis=0)]
    unnamed x29 -> x33, local copies, waits for them, and re-layouts: 7.12 us -> 9.32 us
where the time goes in v4:
time: 346 us; the launch traced here: 343 us
  Pallas kernels  257 us (74%)
  matrix products  35.7 us (10%)
  local copies, waits for them, and re-layouts  31.9 us (9%)
  other arithmetic  17.3 us (5%)
    pallas_call x10, Pallas kernels, transfer(): pl.pallas_call(functools.partial(transfer_kernel, moves), out_shape=[jax....  257 us
    dot_general x8, matrix products, mixed(): return dot(exact, head) + dot(exact, tail)  16.5 us
    unnamed x33, local copies, waits for them, and re-layouts  9.32 us

profile of v4, /device:TPU:0, one launch (start us, length us, event | category | flops | bytes accessed | tf_op | source)
XLA Modules:
  0.0 343.3 jit_solution(4390203402593207861)
XLA Ops:
  3.9 59.3 %shard_map.93 = (bf16[4,1024,256]{2,1,0:T(8,128)(2,1)}, f32[2,2,512,256]{3,2,1,0:T(8,128)}) custom-call(bf16[4,1024,256]{2,1,0:T(8,128)(2,1)} %pad_maximum_fusion.refs_0_, f32[2,512,256]{2,1,0:T(8,128)} %refs_1_.1), custom_call_target="tpu_custom_call" | custom-call | tf_op jit(solution)/shard_map/pallas_call | solution.py:278
  63.2 2.9 copy.61
  66.1 3.0 fusion.6
  72.2 2.9 copy.63
  75.1 32.5 %shard_map.94 = f32[4,1024,128]{2,1,0:T(8,128)} custom-call(f32[4,1024,128]{2,1,0:T(8,128)} %bitcast.96), custom_call_target="tpu_custom_call" | custom-call | tf_op jit(solution)/shard_map/pallas_call | solution.py:278
  113.5 14.1 %shard_map.95 = f32[8,16,1024]{2,1,0:T(8,128)} custom-call(f32[8,16,1024]{2,1,0:T(8,128)} %reshape.60.refs_0_), custom_call_target="tpu_custom_call" | custom-call | tf_op jit(solution)/shard_map/pallas_call | solution.py:278
  129.4 15.5 %shard_map.96 = f32[8,16,1024]{2,1,0:T(8,128)} custom-call(f32[16,1024]{1,0:T(8,128)} %reduce_sum.89.refs_0_), custom_call_target="tpu_custom_call" | custom-call | tf_op jit(solution)/shard_map/pallas_call | solution.py:278
  147.0 2.3 convolution_bitcast_fusion
  150.9 27.1 %shard_map.97 = (f32[4,1024,128]{2,1,0:T(8,128)}, f32[4,32,256]{2,1,0:T(8,128)}) custom-call(f32[1024,128]{1,0:T(8,128)} %fusion.21.refs_0_, f32[4,32,256]{2,1,0:T(8,128)} %dynamic-slice_bitcast_fusion.refs_1_), custom_call_target="tpu_custom_call" | custom-call | tf_op jit(solution)/shard_map/pallas_call | solution.py:278
  179.4 3.0 fusion.2
  182.5 2.7 add_bitcast_fusion
  185.1 3.0 reshape.73
  188.2 3.6 %slice.30 = f32[4,2,40,512]{2,1,0,3:T(2,128)} slice(f32[4,2,128,512]{2,1,0,3:T(2,128)S(1)} %reshape.73), slice={[0:4], [0:2], [88:128], [0:512]} | slice | bytes 1310720 | tf_op jit(solution)/shard_map/slice | solution.py:364
  191.7 3.8 %copy.90.refs_1_ = f32[4,2,40,512]{3,2,1,0:T(8,128)} copy(f32[4,2,40,512]{2,1,0,3:T(2,128)} %slice.30) | data formatting | bytes 1310720
  195.5 2.6 copy.91
  198.2 33.1 %shard_map.98 = (f32[2,4,88,512]{3,2,1,0:T(8,128)}, f32[4,2,40,512]{3,2,1,0:T(8,128)}) custom-call(f32[2,4,88,512]{3,2,1,0:T(8,128)} %bitcast.97, f32[4,2,40,512]{3,2,1,0:T(8,128)} %copy.90.refs_1_), custom_call_target="tpu_custom_call" | custom-call | tf_op jit(solution)/shard_map/pallas_call | solution.py:278
  231.3 2.5 reduce_sum.90.refs_0_
  234.5 16.5 %shard_map.99 = (f32[4,88,512]{2,1,0:T(8,128)}, f32[2,40,512]{2,1,0:T(8,128)}) custom-call(f32[4,88,512]{2,1,0:T(8,128)} %reduce_sum.90.refs_0_, f32[2,40,512]{2,1,0:T(8,128)} %reduce_sum.91.refs_1_), custom_call_target="tpu_custom_call" | custom-call | tf_op jit(solution)/shard_map/pallas_call | solution.py:278
  254.6 17.4 %shard_map.100 = (f32[8,64,256]{2,1,0:T(8,128)}, f32[1,128,512]{2,1,0:T(8,128)}) custom-call(f32[8,64,256]{2,1,0:T(8,128)} %bitcast.101, f32[128,512]{1,0:T(8,128)} %copy-done.9), custom_call_target="tpu_custom_call" | custom-call | tf_op jit(solution)/shard_map/pallas_call | solution.py:278
  273.7 28.2 %shard_map.101 = (f32[4,64,256]{2,1,0:T(8,128)}, f32[4,128,512]{2,1,0:T(8,128)}, f32[8,2,32,256]{3,2,1,0:T(8,128)}) custom-call(f32[64,256]{1,0:T(8,128)} %reduce_sum.94.refs_0_, f32[128,512]{1,0:T(8,128)} %bitcast.105, f32[2,32,256]{2,1,0:T(8,128)} %get-tuple-element.46.refs_2_), custom_call_target="tpu_custom_call" | custom-call | tf_op jit(solution)/shard_map/pallas_call | solution.py:278
  303.5 13.3 %shard_map.102 = f32[8,64,256]{2,1,0:T(8,128)} custom-call(f32[64,256]{1,0:T(8,128)} %reduce_sum.95.refs_0_), custom_call_target="tpu_custom_call" | custom-call | tf_op jit(solution)/shard_map/pallas_call | solution.py:278
  333.8 2.7 copy.78
  336.5 4.2 %fusion.15 = f32[2,512,256]{1,2,0:T(8,128)} fusion(f32[2,512,256]{1,2,0:T(8,128)} %copy.78, f32[2,256,256]{2,1,0:T(8,128)} %bitcast.100, f32[2,512,256]{2,1,0:T(8,128)S(1)} %copy-done.7), kind=kOutput, calls=%fused_computation.21 | convolution fusion | flops 805830656 | bytes 3670016 | tf_op jit(solution)/shard_map/mdk,mkc->mdc/dot_general | solution.py:396
  340.7 2.5 copy.80
  (82 shorter events, 43.2 us)
Async XLA Ops:
  0.6 65.5 %copy-start = (bf16[1024,1024]{1,0:T(8,128)(2,1)S(1)}, bf16[1024,1024]{1,0:T(8,128)(2,1)}, u32[]{:S(2)}) copy-start(bf16[1024,1024]{1,0:T(8,128)(2,1)} %param.6) | copy-start | bytes 6291460
  0.6 1.7 copy-start.8
  66.1 3.0 copy-start.5
  109.4 2.2 copy-start.2
  146.2 3.1 copy-start.3
  149.3 29.4 %copy-start.13 = (f32[2,32,256]{2,1,0:T(8,128)S(1)}, f32[2,32,256]{2,1,0:T(8,128)}, u32[]{:S(2)}) copy-start(f32[2,32,256]{2,1,0:T(8,128)} %param.10) | copy-start | bytes 196612
  149.3 29.4 %copy-start.14 = (f32[2,32,256]{2,1,0:T(8,128)S(1)}, f32[2,32,256]{2,1,0:T(8,128)}, u32[]{:S(2)}) copy-start(f32[2,32,256]{2,1,0:T(8,128)} %param.11) | copy-start | bytes 196612
  179.4 3.0 copy-start.4
  231.3 2.5 copy-start.11
  253.1 1.4 copy-start.9
  316.9 1.5 copy-start.6
  328.0 2.2 copy-start.10
  330.9 2.1 copy-start.12
  332.9 3.6 %copy-start.7 = (f32[2,512,256]{2,1,0:T(8,128)S(1)}, f32[2,512,256]{2,1,0:T(8,128)}, u32[]{:S(2)}) copy-start(f32[2,512,256]{2,1,0:T(8,128)} %refs_1_.1) | copy-start | bytes 3145732
  333.8 9.4 %copy-start.1 = (bf16[1024,1024]{1,0:T(8,128)(2,1)S(1)}, bf16[1024,1024]{1,0:T(8,128)(2,1)}, u32[]{:S(2)}) copy-start(bf16[1024,1024]{1,0:T(8,128)(2,1)} %param.6) | copy-start | bytes 6291460

commit v5 on v4

--- a/solution.py
+++ b/solution.py
@@ -25,8 +25,9 @@
 
 
 class Exchange:
-    def __init__(self, axis, count, scatter, stride=1):
+    def __init__(self, axis, count, scatter, stride=1, pick=None, slot=None):
         self.axis, self.count, self.scatter, self.stride = axis, count, scatter, stride
+        self.pick, self.slot = pick or (lambda ref, peer: ref.at[peer]), slot
 
     def place(self):
         return lax.rem(lax.axis_index(self.axis) // self.stride, self.count)
@@ -36,6 +37,8 @@
         return {self.axis: index + (peer - self.place()) * self.stride}
 
     def shape(self, shape):
+        if self.slot is not None:
+            return (self.count,) + self.slot
         return shape if self.scatter else (self.count,) + shape
 
     def scratch(self):
@@ -56,13 +59,13 @@
 
     def start(self, x_ref, out_ref, own_sem, send_sem, recv_sem):
         me = self.place()
-        own = x_ref.at[me] if self.scatter else x_ref
+        own = self.pick(x_ref, me) if self.scatter else x_ref
         self.copies = [pltpu.make_async_copy(own, out_ref.at[me], own_sem)]
         for hop in range(1, self.count):
             peer = lax.rem(me + hop, self.count)
             self.copies.append(
                 pltpu.make_async_remote_copy(
-                    src_ref=x_ref.at[peer] if self.scatter else x_ref,
+                    src_ref=self.pick(x_ref, peer) if self.scatter else x_ref,
                     dst_ref=out_ref.at[me],
                     send_sem=send_sem.at[hop],
                     recv_sem=recv_sem.at[hop],
@@ -356,12 +359,18 @@
     adam_step = new_first / CORRECT_ONE / (jnp.sqrt(new_second / CORRECT_TWO) + EPSILON)
 
     groups = nf // per
-    part = mixed("tf,jtk->fjk", activations, back).reshape(groups, per, -1, mats * rank)
-    upper = part.shape[2] * 11 // 16 // 8 * 8
+    width = mats * rank
+    back = jnp.transpose(back, (1, 0, 2)).reshape(tokens, width)
+    part = mixed("tf,tk->fk", activations, back).reshape(groups, per, -1, width)
+    depth = part.shape[2]
+    upper = depth * 11 // 16 // 8 * 8
+    lower = depth - upper
     near, far = transfer(
         5,
-        (jnp.swapaxes(part[:, :, :upper], 0, 1), Exchange("fsdp", per, True)),
-        (part[:, :, upper:], Exchange("fsdp", groups, True, per)),
+        (part, Exchange("fsdp", per, True, 1,
+                        lambda ref, peer: ref.at[:, peer, pl.ds(0, upper)], (groups, upper, width))),
+        (part, Exchange("fsdp", groups, True, per,
+                        lambda ref, peer: ref.at[peer, :, pl.ds(upper, lower)], (per, lower, width))),
     )
     near, far = transfer(
         9,

time: 346 us -> 339 us (0.980)
  local copies, waits for them, and re-layouts: 31.9 us -> 24.7 us
    unnamed x33 -> x30, local copies, waits for them, and re-layouts: 9.32 us -> 5.51 us
    slice x1 -> x0, local copies, waits for them, and re-layouts: 3.58 us -> none  [body(): part[:, :, upper:]]
where the time goes in v5:
time: 339 us; the launch traced here: 336 us
  Pallas kernels  257 us (76%)
  matrix products  33.9 us (10%)
  local copies, waits for them, and re-layouts  24.7 us (7%)
  other arithmetic  19.4 us (6%)
    pallas_call x10, Pallas kernels, transfer(): pl.pallas_call(functools.partial(transfer_kernel, moves), out_shape=[jax....  257 us
    dot_general x8, matrix products, mixed(): return dot(exact, head) + dot(exact, tail)  14.7 us

profile of v5, /device:TPU:0, one launch (start us, length us, event | category | flops | bytes accessed | tf_op | source)
XLA Modules:
  0.0 336.2 jit_solution(5284061925246106724)
XLA Ops:
  3.9 59.3 %shard_map.93 = (bf16[4,1024,256]{2,1,0:T(8,128)(2,1)}, f32[2,2,512,256]{3,2,1,0:T(8,128)}) custom-call(bf16[4,1024,256]{2,1,0:T(8,128)(2,1)} %pad_maximum_fusion.refs_0_, f32[2,512,256]{2,1,0:T(8,128)} %refs_1_.1), custom_call_target="tpu_custom_call" | custom-call | tf_op jit(solution)/shard_map/pallas_call | solution.py:281
  63.2 2.9 copy.54
  66.1 3.0 fusion.2
  72.2 2.9 copy.56
  75.1 32.5 %shard_map.94 = f32[4,1024,128]{2,1,0:T(8,128)} custom-call(f32[4,1024,128]{2,1,0:T(8,128)} %bitcast.95), custom_call_target="tpu_custom_call" | custom-call | tf_op jit(solution)/shard_map/pallas_call | solution.py:281
  109.4 2.2 fusion.24
  113.5 14.1 %shard_map.95 = f32[8,16,1024]{2,1,0:T(8,128)} custom-call(f32[8,16,1024]{2,1,0:T(8,128)} %reshape.63.refs_0_), custom_call_target="tpu_custom_call" | custom-call | tf_op jit(solution)/shard_map/pallas_call | solution.py:281
  129.4 15.5 %shard_map.96 = f32[8,16,1024]{2,1,0:T(8,128)} custom-call(f32[16,1024]{1,0:T(8,128)} %reduce_sum.89.refs_0_), custom_call_target="tpu_custom_call" | custom-call | tf_op jit(solution)/shard_map/pallas_call | solution.py:281
  147.0 2.3 convolution_bitcast_fusion
  150.9 27.1 %shard_map.97 = (f32[4,1024,128]{2,1,0:T(8,128)}, f32[4,32,256]{2,1,0:T(8,128)}) custom-call(f32[1024,128]{1,0:T(8,128)} %fusion.15.refs_0_, f32[4,32,256]{2,1,0:T(8,128)} %dynamic-slice_bitcast_fusion.refs_1_), custom_call_target="tpu_custom_call" | custom-call | tf_op jit(solution)/shard_map/pallas_call | solution.py:281
  179.5 2.9 copy.63
  182.3 2.0 fusion.1
  185.6 2.6 add_bitcast_fusion
  188.2 2.9 copy.64
  191.2 33.1 %shard_map.98 = (f32[2,4,88,512]{3,2,1,0:T(8,128)}, f32[4,2,40,512]{3,2,1,0:T(8,128)}) custom-call(f32[4,2,128,512]{3,2,1,0:T(8,128)} %bitcast.93, f32[4,2,128,512]{3,2,1,0:T(8,128)} %bitcast.94), custom_call_target="tpu_custom_call" | custom-call | tf_op jit(solution)/shard_map/pallas_call | solution.py:281
  224.3 2.5 reduce_sum.90.refs_0_
  227.4 16.5 %shard_map.99 = (f32[4,88,512]{2,1,0:T(8,128)}, f32[2,40,512]{2,1,0:T(8,128)}) custom-call(f32[4,88,512]{2,1,0:T(8,128)} %reduce_sum.90.refs_0_, f32[2,40,512]{2,1,0:T(8,128)} %reduce_sum.91.refs_1_), custom_call_target="tpu_custom_call" | custom-call | tf_op jit(solution)/shard_map/pallas_call | solution.py:281
  247.5 17.4 %shard_map.100 = (f32[8,64,256]{2,1,0:T(8,128)}, f32[1,128,512]{2,1,0:T(8,128)}) custom-call(f32[8,64,256]{2,1,0:T(8,128)} %bitcast.99, f32[128,512]{1,0:T(8,128)} %copy-done.8), custom_call_target="tpu_custom_call" | custom-call | tf_op jit(solution)/shard_map/pallas_call | solution.py:281
  266.7 28.2 %shard_map.101 = (f32[4,64,256]{2,1,0:T(8,128)}, f32[4,128,512]{2,1,0:T(8,128)}, f32[8,2,32,256]{3,2,1,0:T(8,128)}) custom-call(f32[64,256]{1,0:T(8,128)} %reduce_sum.94.refs_0_, f32[128,512]{1,0:T(8,128)} %bitcast.104, f32[2,32,256]{2,1,0:T(8,128)} %get-tuple-element.46.refs_2_), custom_call_target="tpu_custom_call" | custom-call | tf_op jit(solution)/shard_map/pallas_call | solution.py:281
  296.5 13.3 %shard_map.102 = f32[8,64,256]{2,1,0:T(8,128)} custom-call(f32[64,256]{1,0:T(8,128)} %reduce_sum.95.refs_0_), custom_call_target="tpu_custom_call" | custom-call | tf_op jit(solution)/shard_map/pallas_call | solution.py:281
  323.9 2.1 convolution_divide_fusion
  326.8 2.7 copy.69
  329.5 4.2 %fusion.9 = f32[2,512,256]{1,2,0:T(8,128)} fusion(f32[2,512,256]{1,2,0:T(8,128)} %copy.69, f32[2,256,256]{2,1,0:T(8,128)} %bitcast.98, f32[2,512,256]{2,1,0:T(8,128)S(1)} %copy-done.6), kind=kOutput, calls=%fused_computation.17 | convolution fusion | flops 805830656 | bytes 3670016 | tf_op jit(solution)/shard_map/mdk,mkc->mdc/dot_general | solution.py:405
  333.7 2.5 copy.71
  (79 shorter events, 40.3 us)
Async XLA Ops:
  0.6 65.5 %copy-start = (bf16[1024,1024]{1,0:T(8,128)(2,1)S(1)}, bf16[1024,1024]{1,0:T(8,128)(2,1)}, u32[]{:S(2)}) copy-start(bf16[1024,1024]{1,0:T(8,128)(2,1)} %param.6) | copy-start | bytes 6291460
  0.6 1.7 copy-start.7
  66.1 3.0 copy-start.4
  109.4 2.2 copy-start.2
  146.2 3.1 copy-start.3
  149.3 29.4 %copy-start.12 = (f32[2,32,256]{2,1,0:T(8,128)S(1)}, f32[2,32,256]{2,1,0:T(8,128)}, u32[]{:S(2)}) copy-start(f32[2,32,256]{2,1,0:T(8,128)} %param.10) | copy-start | bytes 196612
  149.3 29.4 %copy-start.13 = (f32[2,32,256]{2,1,0:T(8,128)S(1)}, f32[2,32,256]{2,1,0:T(8,128)}, u32[]{:S(2)}) copy-start(f32[2,32,256]{2,1,0:T(8,128)} %param.11) | copy-start | bytes 196612
  224.2 2.5 copy-start.10
  246.1 1.4 copy-start.8
  309.8 1.5 copy-start.5
  320.9 2.2 copy-start.9
  323.9 2.1 copy-start.11
  325.9 3.6 %copy-start.6 = (f32[2,512,256]{2,1,0:T(8,128)S(1)}, f32[2,512,256]{2,1,0:T(8,128)}, u32[]{:S(2)}) copy-start(f32[2,512,256]{2,1,0:T(8,128)} %refs_1_.1) | copy-start | bytes 3145732
  326.8 9.4 %copy-start.1 = (bf16[1024,1024]{1,0:T(8,128)(2,1)S(1)}, bf16[1024,1024]{1,0:T(8,128)(2,1)}, u32[]{:S(2)}) copy-start(bf16[1024,1024]{1,0:T(8,128)(2,1)} %param.6) | copy-start | bytes 6291460
